TPU v7x, 256 devices: a whole 4x4x8 slice. The times are simulated.
256 devices in a mesh: seq: 64 (over y, x, z_hi, core), fsdp: 4 (over z_lo).
Axes of the slice: x: 4, y: 4, z: 8 (z_hi: 2, z_lo: 4; z = z_hi * 4 + z_lo), core: 2. Of those that a mesh axis runs over, the one named last changes fastest.
Arguments:
- tokens: bfloat16 [40960, 5120], P('seq', 'fsdp'), may hold values from -24 to 24
- w_local: bfloat16 [5120, 3, 1536], P('seq', None, 'fsdp'), may hold values from -0.078125 to 0.078125
- w_strided: bfloat16 [5120, 3, 1024], P('seq', None, 'fsdp'), may hold values from -0.078125 to 0.078125
- valid: int32 [64, 640], P('seq'), may hold values 0 or 1
- band_reach: int32 [12], P('fsdp'), may hold values from 1 to 4, as said below
Outputs:
- out_local: bfloat16 [40960, 1536], P('seq', 'fsdp')
- out_strided: bfloat16 [40960, 1024], P('seq', 'fsdp')
Inputs may be any that keep to these rules, and one draw needn't show every extreme that they name: Query block b of local head h sees band blocks b - band_reach[h] to b.
All inputs are finite; a program needn't handle non-finite values. No bound on the sum of `valid` on one device may be relied on, other than what follows from the above.
Results may differ from a plain program's by a relative error of at most 0.012.
The roundings to bfloat16 on the way count: a program that leaves them out, or rounds other values in their place, can miss the bound.
Values may be sent and summed in bfloat16 or wider, within the bound.
No kernel may reach another device: no remote copies, remote signals or barrier semaphores. Data moves between devices by JAX's collectives and lax.ppermute only.
A program may use at most 128 MiB of HBM per device.

v0:
```python
import math
import jax
import jax.numpy as jnp
from jax import lax
from jax.sharding import PartitionSpec as P

HD = 128
BLK = 128


def local_attend(qkv_day, valid_day, reach, head_size):
    query = qkv_day[:, 0]
    keys = qkv_day[:, 1]
    values = qkv_day[:, 2]
    seconds = qkv_day.shape[0]
    scores = jnp.einsum(
        "qhc,khc->hqk", query, keys, preferred_element_type=jnp.float32
    ) / math.sqrt(head_size)
    position = jnp.arange(seconds)
    causal = position[None, :] <= position[:, None]
    block = position // BLK
    band = block[None, None, :] >= block[None, :, None] - reach[:, None, None]
    seen = (valid_day[None, :] > 0) | (position[None, :] == position[:, None])
    allowed = causal[None] & band & seen[None]
    scores = jnp.where(allowed, scores, -jnp.inf)
    row_max = jnp.max(scores, axis=-1, keepdims=True)
    expo = jnp.exp(scores - row_max)
    probs = (expo / jnp.sum(expo, axis=-1, keepdims=True)).astype(jnp.bfloat16)
    result = jnp.einsum("hqk,khc->qhc", probs, values, preferred_element_type=jnp.float32)
    return result.astype(jnp.bfloat16).reshape(seconds, -1)


def body(tokens, w_local, w_strided, valid, band_reach):
    gathered = lax.all_gather(tokens, "fsdp", axis=1, tiled=True)
    seconds = gathered.shape[0]
    local_cols = w_local.shape[2]
    strided_cols = w_strided.shape[2]
    head_size = HD
    peers = lax.axis_size("seq")
    per_peer = seconds // peers

    def add_rows(piece):
        rows = piece.shape[0]
        return jnp.dot(gathered, piece.reshape(rows, -1), preferred_element_type=jnp.float32)

    acc_local = add_rows(lax.all_gather(w_local, "seq", axis=0, tiled=True))
    acc_strided = add_rows(lax.all_gather(w_strided, "seq", axis=0, tiled=True))
    packed = acc_strided.astype(jnp.bfloat16).reshape(1, peers, per_peer, 3 * strided_cols)
    marks = valid.astype(jnp.bfloat16).reshape(1, peers, per_peer)
    strided_packed = lax.all_to_all(packed, "seq", split_axis=1, concat_axis=0, tiled=True)
    strided_marks = lax.all_to_all(marks, "seq", split_axis=1, concat_axis=0, tiled=True)
    days = strided_packed.shape[0]
    count = strided_packed.shape[2]
    heads = strided_cols // head_size
    split_up = strided_packed.reshape(days, count, 3, heads, head_size)
    query = split_up[:, :, 0]
    keys = split_up[:, :, 1]
    values = split_up[:, :, 2]
    scores = jnp.einsum(
        "dshc,eshc->shde", query, keys, preferred_element_type=jnp.float32
    ) / math.sqrt(head_size)
    day = jnp.arange(days)
    causal = day[None, :] <= day[:, None]
    same = day[None, :] == day[:, None]
    seen = jnp.transpose(strided_marks[:, 0, :]) > 0
    allowed = causal[None, None] & (seen[:, None, None, :] | same[None, None])
    scores = jnp.where(allowed, scores, -jnp.inf)
    row_max = jnp.max(scores, axis=-1, keepdims=True)
    expo = jnp.exp(scores - row_max)
    probs = (expo / jnp.sum(expo, axis=-1, keepdims=True)).astype(jnp.bfloat16)
    result = jnp.einsum("shde,eshc->dshc", probs, values, preferred_element_type=jnp.float32)
    result = result.astype(jnp.bfloat16).reshape(days, 1, count, strided_cols)
    result = lax.all_to_all(result, "seq", split_axis=0, concat_axis=1, tiled=True)
    out_strided = result.reshape(seconds, strided_cols)
    qkv_local = acc_local.astype(jnp.bfloat16).reshape(
        seconds, 3, local_cols // head_size, head_size
    )
    out_local = local_attend(qkv_local, valid[0], band_reach, head_size)
    return (out_local, out_strided)


def solution(mesh):
    in_specs = (
        P("seq", "fsdp"),
        P("seq", None, "fsdp"),
        P("seq", None, "fsdp"),
        P("seq", None),
        P("fsdp"),
    )
    out_specs = (P("seq", "fsdp"), P("seq", "fsdp"))
    return jax.shard_map(body, mesh=mesh, in_specs=in_specs, out_specs=out_specs, check_vma=False)
```

profile of v0, /device:TPU:1, one launch (start us, length us, event | category | flops | bytes accessed | tf_op | source)
XLA Modules:
  0.0 441.7 jit_solution(410772100073191428)
XLA Ops:
  7.2 0.0 all-gather.8.cloned.1.call-start
  7.2 0.7 all-gather.8.cloned.1.call-update
  7.9 0.0 all-gather.4.cloned.1.call-start
  7.9 0.7 all-gather.4.cloned.1.call-update
  8.6 0.0 all-gather.6.cloned.1.call-start
  8.7 0.7 all-gather.6.cloned.1.call-update
  9.4 0.7 convert_reduce_fusion
  10.1 0.8 reshape.195
  10.9 15.6 %all-to-all-start.1 = ((bf16[1,64,10]{2,0,1:T(2,128)(2,1)}), bf16[1,64,10]{2,0,1:T(2,128)(2,1)S(1)}, u32[]{:S(2)}, u32[]{:S(2)}) async-start(bf16[1,64,10]{2,0,1:T(2,128)(2,1)} %reshape.195), calls=%async_computation.1 | async-start | bytes 65536 | tf_op jit(solution)/shard_map/all_to_all | solution.py:51
  26.5 100.5 %all-gather.8.cloned.1.call-done = bf16[5120,3,256]{2,0,1:T(8,128)(2,1)} async-done(((bf16[80,3,256]{2,0,1:T(8,128)(2,1)}), bf16[5120,3,256]{2,0,1:T(8,128)(2,1)}) %all-gather.8.cloned.1.call-update) | async-done | bytes 7864336 | tf_op jit(solution)/shard_map/all_gather | solution.py:47
  127.0 11.0 %copy.51 = bf16[5120,3,256]{0,2,1:T(8,128)(2,1)} copy(bf16[5120,3,256]{2,0,1:T(8,128)(2,1)} %all-gather.8.cloned.1.call-done) | data formatting | bytes 15728640 | tf_op jit(solution)/shard_map/all_gather | solution.py:47
  138.0 107.3 %all-gather.4.cloned.1.call-done = bf16[640,5120]{1,0:T(8,128)(2,1)} async-done(((bf16[640,1280]{1,0:T(8,128)(2,1)}), bf16[640,5120]{1,0:T(8,128)(2,1)}) %all-gather.4.cloned.1.call-update) | async-done | bytes 6553616 | tf_op jit(solution)/shard_map/all_gather | solution.py:34
  245.3 9.7 %convolution_convert_fusion.1 = bf16[640,768]{1,0:T(8,128)(2,1)S(1)} fusion(bf16[640,5120]{1,0:T(8,128)(2,1)} %all-gather.4.cloned.1.call-done, bf16[5120,768]{0,1:T(8,128)(2,1)} %bitcast.60), kind=kOutput, calls=%fused_computation.17 | convolution fusion | flops 5033656320 | bytes 15400960 | tf_op jit(solution)/shard_map/dot_general | solution.py:44
  255.0 0.0 copy-start
  255.0 1.4 reshape.189
  256.4 0.0 all-to-all-done.1
  256.4 11.4 %all-to-all-start = ((bf16[1,64,10,768]{3,2,0,1:T(8,128)(2,1)}), bf16[1,64,10,768]{3,2,0,1:T(8,128)(2,1)S(1)}, u32[]{:S(2)}, u32[]{:S(2)}) async-start(bf16[1,64,10,768]{3,2,0,1:T(8,128)(2,1)} %bitcast.8), calls=%async_computation | async-start | bytes 3145728 | tf_op jit(solution)/shard_map/all_to_all | solution.py:50
  267.9 0.0 copy-done
  267.9 0.1 copy.56
  268.0 0.2 or_and_fusion
  268.2 37.1 %all-to-all-done = bf16[1,64,10,768]{3,2,0,1:T(8,128)(2,1)S(1)} async-done(((bf16[1,64,10,768]{3,2,0,1:T(8,128)(2,1)}), bf16[1,64,10,768]{3,2,0,1:T(8,128)(2,1)S(1)}, u32[]{:S(2)}, u32[]{:S(2)}) %all-to-all-start) | async-done | bytes 983072 | tf_op jit(solution)/shard_map/all_to_all | solution.py:50
  305.3 0.6 reshape.194
  305.9 0.0 copy-start.1
  305.9 0.7 fusion.30
  306.6 0.3 fusion.14
  306.9 0.2 fusion.32
  307.1 0.3 fusion.15
  307.4 0.3 copy.69
  307.8 1.0 reshape.196
  308.8 4.4 all-to-all-start.2
  313.2 0.1 iota_compare_fusion.1
  313.3 0.0 copy-done.1
  313.3 0.1 broadcast_subtract_fusion
  313.4 0.9 fusion.10
  314.3 14.2 %all-to-all-done.2 = bf16[64,1,10,256]{3,2,1,0:T(8,128)(2,1)S(1)} async-done(((bf16[64,1,10,256]{3,2,1,0:T(8,128)(2,1)}), bf16[64,1,10,256]{3,2,1,0:T(8,128)(2,1)S(1)}, u32[]{:S(2)}, u32[]{:S(2)}) %all-to-all-start.2) | async-done | bytes 327712 | tf_op jit(solution)/shard_map/all_to_all | solution.py:73
  328.5 0.8 reshape.193
  329.4 68.7 %all-gather.6.cloned.1.call-done = bf16[5120,3,384]{2,0,1:T(8,128)(2,1)} async-done(((bf16[80,3,384]{2,0,1:T(8,128)(2,1)}), bf16[5120,3,384]{2,0,1:T(8,128)(2,1)}) %all-gather.6.cloned.1.call-update) | async-done | bytes 11796496 | tf_op jit(solution)/shard_map/all_gather | solution.py:46
  398.1 15.0 %copy.46 = bf16[5120,3,384]{0,2,1:T(8,128)(2,1)} copy(bf16[5120,3,384]{2,0,1:T(8,128)(2,1)} %all-gather.6.cloned.1.call-done) | data formatting | bytes 23592960 | tf_op jit(solution)/shard_map/all_gather | solution.py:46
  413.1 12.7 %convolution_convert_fusion = bf16[640,1152]{1,0:T(8,128)(2,1)S(1)} fusion(bf16[640,5120]{1,0:T(8,128)(2,1)} %all-gather.4.cloned.1.call-done, bf16[5120,1152]{0,1:T(8,128)(2,1)} %bitcast.59), kind=kOutput, calls=%fused_computation.5 | convolution fusion | flops 7550484480 | bytes 19824640 | tf_op jit(solution)/shard_map/dot_general | solution.py:44
  425.8 0.9 copy.47
  426.7 3.5 fusion.31
  430.2 4.0 fusion.12
  434.2 1.0 copy.62
  (4 shorter events, 0.1 us)
Async XLA Ops:
  7.2 119.8 %all-gather.8.cloned.1.call-start = ((), (), s32[]{:S(2)}) async-start(), calls=%async_computation.5 | async-start | bytes 7987200 | tf_op jit(solution)/shard_map/all_gather | solution.py:47
  7.9 237.4 %all-gather.4.cloned.1.call-start = ((), (), s32[]{:S(2)}) async-start(), calls=%async_computation.3 | async-start | bytes 8192000 | tf_op jit(solution)/shard_map/all_gather | solution.py:34
  8.6 389.4 %all-gather.6.cloned.1.call-start = ((), (), s32[]{:S(2)}) async-start(), calls=%async_computation.4 | async-start | bytes 11980800 | tf_op jit(solution)/shard_map/all_gather | solution.py:46
  10.9 245.6 %all-to-all-start.1 = ((bf16[1,64,10]{2,0,1:T(2,128)(2,1)}), bf16[1,64,10]{2,0,1:T(2,128)(2,1)S(1)}, u32[]{:S(2)}, u32[]{:S(2)}) async-start(bf16[1,64,10]{2,0,1:T(2,128)(2,1)} %reshape.195), calls=%async_computation.1 | async-start | bytes 65536 | tf_op jit(solution)/shard_map/all_to_all | solution.py:51
  255.0 12.9 %copy-start = (s32[1,640]{1,0:T(1,128)S(1)}, s32[1,640]{1,0:T(1,128)}, u32[]{:S(2)}) copy-start(s32[1,640]{1,0:T(1,128)} %param.8) | copy-start | bytes 7684
  256.4 48.9 %all-to-all-start = ((bf16[1,64,10,768]{3,2,0,1:T(8,128)(2,1)}), bf16[1,64,10,768]{3,2,0,1:T(8,128)(2,1)S(1)}, u32[]{:S(2)}, u32[]{:S(2)}) async-start(bf16[1,64,10,768]{3,2,0,1:T(8,128)(2,1)} %bitcast.8), calls=%async_computation | async-start | bytes 3145728 | tf_op jit(solution)/shard_map/all_to_all | solution.py:50
  305.9 7.4 %copy-start.1 = (s32[3]{0:T(128)S(1)}, s32[3]{0:T(128)}, u32[]{:S(2)}) copy-start(s32[3]{0:T(128)} %param.9) | copy-start | bytes 40
  308.8 19.7 %all-to-all-start.2 = ((bf16[64,1,10,256]{3,2,1,0:T(8,128)(2,1)}), bf16[64,1,10,256]{3,2,1,0:T(8,128)(2,1)S(1)}, u32[]{:S(2)}, u32[]{:S(2)}) async-start(bf16[64,1,10,256]{3,2,1,0:T(8,128)(2,1)} %reshape.196), calls=%async_computation.2 | async-start | bytes 1048576 | tf_op jit(solution)/shard_map/all_to_all | solution.py:73
Sparse Core Ops, SparseCore 0:
  11.5 115.4 all-gather.7
  128.8 116.4 all-gather.3
  248.8 149.2 all-gather.5
where the time goes:
time: 443 us; the launch traced here: 442 us
  waiting for transfers between devices  330 us (74%)
  local copies, waits for them, and re-layouts  33.7 us (8%)
  starting transfers between devices  31.5 us (7%)
  matrix products  30.5 us (7%)
  between operations  13.9 us (3%)
    all_gather x1, waiting for transfers between devices, body(): gathered = lax.all_gather(tokens, 'fsdp', axis=1, tiled=True)  107 us
    all_gather x1, waiting for transfers between devices, body(): acc_strided = add_rows(lax.all_gather(w_strided, 'seq', axis=0, tiled=True))  101 us
    all_gather x1, waiting for transfers between devices, body(): acc_local = add_rows(lax.all_gather(w_local, 'seq', axis=0, tiled=True))  68.7 us
    all_to_all x1, waiting for transfers between devices, body(): lax.all_to_all(packed, 'seq', split_axis=1, concat_axis=0, tiled=True)  37.1 us
    dot_general x2, matrix products, add_rows(): jnp.dot(gathered, piece.reshape(rows, -1), preferred_element_type=jnp.flo...  22.4 us
    all_to_all x1, starting transfers between devices, body(): lax.all_to_all(marks, 'seq', split_axis=1, concat_axis=0, tiled=True)  15.6 us
    all_gather x1, local copies, waits for them, and re-layouts, body(): acc_local = add_rows(lax.all_gather(w_local, 'seq', axis=0, tiled=True))  15 us
    all_to_all x1, waiting for transfers between devices, body(): lax.all_to_all(result, 'seq', split_axis=0, concat_axis=1, tiled=True)  14.2 us
  transfers between devices with their start and end apart: 6, of which 5 were waited for; matrix products, arithmetic and copies ran while one was open for 7% of the time, Pallas kernels for 0%

commit v1 on v0

--- a/solution.py
+++ b/solution.py
@@ -3,9 +3,17 @@
 import jax.numpy as jnp
 from jax import lax
 from jax.sharding import PartitionSpec as P
+from jax.lax import all_to_all, axis_size
 
 HD = 128
 BLK = 128
+
+
+def serve_flows(vec, array_dim, pos_dim):
+    return jnp.concatenate(
+        all_to_all(jnp.stack(jnp.split(vec, axis_size("seq"), axis=array_dim)), "seq", 0, 0),
+        pos_dim,
+    )
 
 
 def local_attend(qkv_day, valid_day, reach, head_size):
@@ -70,7 +78,7 @@
     probs = (expo / jnp.sum(expo, axis=-1, keepdims=True)).astype(jnp.bfloat16)
     result = jnp.einsum("shde,eshc->dshc", probs, values, preferred_element_type=jnp.float32)
     result = result.astype(jnp.bfloat16).reshape(days, 1, count, strided_cols)
-    result = lax.all_to_all(result, "seq", split_axis=0, concat_axis=1, tiled=True)
+    result = serve_flows(result, 0, 1)
     out_strided = result.reshape(seconds, strided_cols)
     qkv_local = acc_local.astype(jnp.bfloat16).reshape(
         seconds, 3, local_cols // head_size, head_size

time: 443 us -> 450 us (1.016)
  local copies, waits for them, and re-layouts: 33.7 us -> 73.8 us
  waiting for transfers between devices: 330 us -> 297 us
    all_gather x1, waiting for transfers between devices: 68.7 us -> 22.1 us  [body(): acc_local = add_rows(lax.all_gather(w_local, 'seq', axis=0, tiled=True))]
    unnamed x5 -> x68, local copies, waits for them, and re-layouts: 1.01 us -> 38.5 us
    all_to_all x1, waiting for transfers between devices: 14.2 us -> 27.6 us  [serve_flows(): all_to_all(jnp.stack(jnp.split(vec, axis_size('seq'), axis=array_dim)), '...]
  transfers between devices with their start and end apart: 6 -> 6, of which waited for: 5 -> 5; matrix products, arithmetic and copies ran while one was open for 7% -> 15% of each run, Pallas kernels for 0% -> 0%
where the time goes in v1:
time: 450 us; the launch traced here: 449 us
  waiting for transfers between devices  297 us (66%)
  local copies, waits for them, and re-layouts  73.8 us (16%)
  starting transfers between devices  31.5 us (7%)
  matrix products  30.5 us (7%)
  between operations  14.1 us (3%)
    all_gather x1, waiting for transfers between devices, body(): gathered = lax.all_gather(tokens, 'fsdp', axis=1, tiled=True)  107 us
    all_gather x1, waiting for transfers between devices, body(): acc_strided = add_rows(lax.all_gather(w_strided, 'seq', axis=0, tiled=True))  101 us
    unnamed x68, local copies, waits for them, and re-layouts  38.5 us
    all_to_all x1, waiting for transfers between devices, body(): lax.all_to_all(packed, 'seq', split_axis=1, concat_axis=0, tiled=True)  37.1 us
    all_to_all x1, waiting for transfers between devices, serve_flows(): all_to_all(jnp.stack(jnp.split(vec, axis_size('seq'), axis=array_dim)), '...  27.6 us
    dot_general x2, matrix products, add_rows(): jnp.dot(gathered, piece.reshape(rows, -1), preferred_element_type=jnp.flo...  22.4 us
    all_gather x1, waiting for transfers between devices, body(): acc_local = add_rows(lax.all_gather(w_local, 'seq', axis=0, tiled=True))  22.1 us
    all_to_all x1, starting transfers between devices, body(): lax.all_to_all(marks, 'seq', split_axis=1, concat_axis=0, tiled=True)  15.6 us
  transfers between devices with their start and end apart: 6, of which 5 were waited for; matrix products, arithmetic and copies ran while one was open for 15% of the time, Pallas kernels for 0%

profile of v1, /device:TPU:1, one launch (start us, length us, event | category | flops | bytes accessed | tf_op | source)
XLA Modules:
  0.0 448.7 jit_solution(4240641726672757323)
XLA Ops:
  7.2 0.7 all-gather.8.cloned.1.call-update
  7.9 0.7 all-gather.4.cloned.1.call-update
  8.7 0.7 all-gather.6.cloned.1.call-update
  9.4 0.7 convert_reduce_fusion
  10.1 0.8 reshape.312
  10.9 15.6 %all-to-all-start.1 = ((bf16[1,64,10]{2,0,1:T(2,128)(2,1)}), bf16[1,64,10]{2,0,1:T(2,128)(2,1)S(1)}, u32[]{:S(2)}, u32[]{:S(2)}) async-start(bf16[1,64,10]{2,0,1:T(2,128)(2,1)} %reshape.312), calls=%async_computation.1 | async-start | bytes 65536 | tf_op jit(solution)/shard_map/all_to_all | solution.py:59
  26.5 100.5 %all-gather.8.cloned.1.call-done = bf16[5120,3,256]{2,0,1:T(8,128)(2,1)} async-done(((bf16[80,3,256]{2,0,1:T(8,128)(2,1)}), bf16[5120,3,256]{2,0,1:T(8,128)(2,1)}) %all-gather.8.cloned.1.call-update) | async-done | bytes 7864336 | tf_op jit(solution)/shard_map/all_gather | solution.py:55
  127.0 11.0 %copy.47 = bf16[5120,3,256]{0,2,1:T(8,128)(2,1)} copy(bf16[5120,3,256]{2,0,1:T(8,128)(2,1)} %all-gather.8.cloned.1.call-done) | data formatting | bytes 15728640 | tf_op jit(solution)/shard_map/all_gather | solution.py:55
  138.0 107.3 %all-gather.4.cloned.1.call-done = bf16[640,5120]{1,0:T(8,128)(2,1)} async-done(((bf16[640,1280]{1,0:T(8,128)(2,1)}), bf16[640,5120]{1,0:T(8,128)(2,1)}) %all-gather.4.cloned.1.call-update) | async-done | bytes 6553616 | tf_op jit(solution)/shard_map/all_gather | solution.py:42
  245.3 9.7 %convolution_convert_fusion.1 = bf16[640,768]{1,0:T(8,128)(2,1)S(1)} fusion(bf16[640,5120]{1,0:T(8,128)(2,1)} %all-gather.4.cloned.1.call-done, bf16[5120,768]{0,1:T(8,128)(2,1)} %bitcast.60), kind=kOutput, calls=%fused_computation.17 | convolution fusion | flops 5033656320 | bytes 15400960 | tf_op jit(solution)/shard_map/dot_general | solution.py:52
  255.0 1.4 reshape.308
  256.4 11.4 %all-to-all-start = ((bf16[1,64,10,768]{3,2,0,1:T(8,128)(2,1)}), bf16[1,64,10,768]{3,2,0,1:T(8,128)(2,1)S(1)}, u32[]{:S(2)}, u32[]{:S(2)}) async-start(bf16[1,64,10,768]{3,2,0,1:T(8,128)(2,1)} %bitcast.8), calls=%async_computation | async-start | bytes 3145728 | tf_op jit(solution)/shard_map/all_to_all | solution.py:58
  268.2 37.1 %all-to-all-done = bf16[1,64,10,768]{3,2,0,1:T(8,128)(2,1)S(1)} async-done(((bf16[1,64,10,768]{3,2,0,1:T(8,128)(2,1)}), bf16[1,64,10,768]{3,2,0,1:T(8,128)(2,1)S(1)}, u32[]{:S(2)}, u32[]{:S(2)}) %all-to-all-start) | async-done | bytes 983072 | tf_op jit(solution)/shard_map/all_to_all | solution.py:58
  305.9 0.7 fusion.30
  307.8 0.6 slice_reduce_fusion.38
  308.8 0.6 slice_reduce_fusion
  309.5 0.6 slice_reduce_fusion.19
  311.5 0.6 constant_dynamic-update-slice_fusion.62
  314.5 0.6 constant_dynamic-update-slice_fusion.57
  315.7 0.6 constant_dynamic-update-slice_fusion.55
  319.3 0.6 constant_dynamic-update-slice_fusion.49
  319.9 0.6 constant_dynamic-update-slice_fusion.48
  321.1 0.6 constant_dynamic-update-slice_fusion.46
  322.8 0.6 constant_dynamic-update-slice_fusion.43
  323.4 0.6 constant_dynamic-update-slice_fusion.42
  326.4 0.6 constant_dynamic-update-slice_fusion.37
  327.0 0.6 constant_dynamic-update-slice_fusion.36
  328.8 0.6 constant_dynamic-update-slice_fusion.33
  329.4 0.6 constant_dynamic-update-slice_fusion.32
  330.6 0.6 constant_dynamic-update-slice_fusion.30
  333.0 0.6 constant_dynamic-update-slice_fusion.26
  334.2 0.6 constant_dynamic-update-slice_fusion.24
  337.1 0.6 constant_dynamic-update-slice_fusion.19
  340.7 0.6 constant_dynamic-update-slice_fusion.13
  342.5 0.6 constant_dynamic-update-slice_fusion.10
  347.8 0.6 constant_dynamic-update-slice_fusion.1
  348.4 0.6 constant_dynamic-update-slice_fusion
  349.0 4.4 all-to-all-start.2
  353.7 0.9 fusion.10
  354.6 27.6 %all-to-all-done.2 = bf16[64,1,1,10,256]{4,3,2,1,0:T(8,128)(2,1)S(1)} async-done(((bf16[64,1,1,10,256]{4,3,2,1,0:T(8,128)(2,1)}), bf16[64,1,1,10,256]{4,3,2,1,0:T(8,128)(2,1)S(1)}, u32[]{:S(2)}, u32[]{:S(2)}) %all-to-all-start.2) | async-done | bytes 327712 | tf_op jit(solution)/shard_map/all_to_all | solution.py:14
  382.2 0.8 reshape_reshape.3
  383.0 22.1 %all-gather.6.cloned.1.call-done = bf16[5120,3,384]{2,0,1:T(8,128)(2,1)} async-done(((bf16[80,3,384]{2,0,1:T(8,128)(2,1)}), bf16[5120,3,384]{2,0,1:T(8,128)(2,1)}) %all-gather.6.cloned.1.call-update) | async-done | bytes 11796496 | tf_op jit(solution)/shard_map/all_gather | solution.py:54
  405.1 15.0 %copy.42 = bf16[5120,3,384]{0,2,1:T(8,128)(2,1)} copy(bf16[5120,3,384]{2,0,1:T(8,128)(2,1)} %all-gather.6.cloned.1.call-done) | data formatting | bytes 23592960 | tf_op jit(solution)/shard_map/all_gather | solution.py:54
  420.1 12.7 %convolution_convert_fusion = bf16[640,1152]{1,0:T(8,128)(2,1)S(1)} fusion(bf16[640,5120]{1,0:T(8,128)(2,1)} %all-gather.4.cloned.1.call-done, bf16[5120,1152]{0,1:T(8,128)(2,1)} %bitcast.59), kind=kOutput, calls=%fused_computation.5 | convolution fusion | flops 7550484480 | bytes 19824640 | tf_op jit(solution)/shard_map/dot_general | solution.py:52
  432.8 0.9 copy.43
  433.7 3.5 fusion.31
  437.2 4.0 fusion.12
  441.2 1.0 copy.56
  (129 shorter events, 29.6 us)
Async XLA Ops:
  7.2 119.8 %all-gather.8.cloned.1.call-start = ((), (), s32[]{:S(2)}) async-start(), calls=%async_computation.5 | async-start | bytes 7987200 | tf_op jit(solution)/shard_map/all_gather | solution.py:55
  7.9 237.4 %all-gather.4.cloned.1.call-start = ((), (), s32[]{:S(2)}) async-start(), calls=%async_computation.3 | async-start | bytes 8192000 | tf_op jit(solution)/shard_map/all_gather | solution.py:42
  8.6 396.4 %all-gather.6.cloned.1.call-start = ((), (), s32[]{:S(2)}) async-start(), calls=%async_computation.4 | async-start | bytes 11980800 | tf_op jit(solution)/shard_map/all_gather | solution.py:54
  10.9 245.6 %all-to-all-start.1 = ((bf16[1,64,10]{2,0,1:T(2,128)(2,1)}), bf16[1,64,10]{2,0,1:T(2,128)(2,1)S(1)}, u32[]{:S(2)}, u32[]{:S(2)}) async-start(bf16[1,64,10]{2,0,1:T(2,128)(2,1)} %reshape.312), calls=%async_computation.1 | async-start | bytes 65536 | tf_op jit(solution)/shard_map/all_to_all | solution.py:59
  255.0 12.9 %copy-start = (s32[1,640]{1,0:T(1,128)S(1)}, s32[1,640]{1,0:T(1,128)}, u32[]{:S(2)}) copy-start(s32[1,640]{1,0:T(1,128)} %param.8) | copy-start | bytes 7684
  256.4 48.9 %all-to-all-start = ((bf16[1,64,10,768]{3,2,0,1:T(8,128)(2,1)}), bf16[1,64,10,768]{3,2,0,1:T(8,128)(2,1)S(1)}, u32[]{:S(2)}, u32[]{:S(2)}) async-start(bf16[1,64,10,768]{3,2,0,1:T(8,128)(2,1)} %bitcast.8), calls=%async_computation | async-start | bytes 3145728 | tf_op jit(solution)/shard_map/all_to_all | solution.py:58
  306.6 47.0 %copy-start.1 = (s32[3]{0:T(128)S(1)}, s32[3]{0:T(128)}, u32[]{:S(2)}) copy-start(s32[3]{0:T(128)} %param.9) | copy-start | bytes 40
  349.0 33.1 %all-to-all-start.2 = ((bf16[64,1,1,10,256]{4,3,2,1,0:T(8,128)(2,1)}), bf16[64,1,1,10,256]{4,3,2,1,0:T(8,128)(2,1)S(1)}, u32[]{:S(2)}, u32[]{:S(2)}) async-start(bf16[64,1,1,10,256]{4,3,2,1,0:T(8,128)(2,1)} %constant_dynamic-update-slice_fusion), calls=%async_computation.2 | async-start | bytes 1048576 | tf_op jit(solution)/shard_map/all_to_all | solution.py:14
Sparse Core Ops, SparseCore 0:
  11.5 115.4 all-gather.7
  128.8 116.4 all-gather.3
  248.8 156.2 all-gather.5
